TPU v7x, 256 devices: a whole 4x4x8 slice. The times are simulated.
256 devices in a mesh: rep: 32 (over y, z), shard: 8 (over x, core).
Axes of the slice: x: 4, y: 4, z: 8, core: 2. Of those that a mesh axis runs over, the one named last changes fastest.
Arguments:
- gradient: bfloat16 [32, 1024, 4096], P('rep', None, 'shard'), may hold values from -16 to 16
- feedback: bfloat16 [32, 1024, 4096], P('rep', None, 'shard'), may hold values from -4 to 4
- warm_start: float32 [1024, 64], replicated, may hold values from -6 to 6
- master: float32 [1024, 4096], P('rep', 'shard'), may hold values from -4 to 4
- moment: float32 [1024, 4096], P('rep', 'shard'), may hold values from -1.5 to 1.5
- second: float32 [1024, 4096], P('rep', 'shard'), may hold values from 0.005 to 0.5
Outputs:
- new_feedback: bfloat16 [32, 1024, 4096], P('rep', None, 'shard')
- weights: bfloat16 [1024, 4096], P(None, 'shard')
- master_out: float32 [1024, 4096], P('rep', 'shard')
- moment_out: float32 [1024, 4096], P('rep', 'shard')
- second_out: float32 [1024, 4096], P('rep', 'shard')
- right_factor: float32 [1024, 64], replicated
All inputs are finite; a program needn't handle non-finite values.
Results may differ from a plain program's by a relative error of at most 0.001.
Values may be sent and summed in bfloat16 or wider, within the bound.
No kernel may reach another device: no remote copies, remote signals or barrier semaphores. Data moves between devices by JAX's collectives and lax.ppermute only.
A program may use at most 64 MiB of HBM per device.

v0:
```python
import jax
import jax.numpy as jnp
from jax import lax
from jax.sharding import PartitionSpec as P

HIGHEST = lax.Precision.HIGHEST
beta_one = 0.9
beta_two = 0.95
learn_rate = 0.02
decay_rate = 0.1
adam_eps = 1e-08
ridge_rate = 1e-06


def lower_inverse(gram):
    matrix_order = gram.shape[0]
    identity = jnp.eye(matrix_order, dtype=jnp.float32)
    ridge_term = ridge_rate * jnp.trace(gram) / matrix_order
    cholesky_lower = jnp.linalg.cholesky(gram + ridge_term * identity)
    return jax.scipy.linalg.solve_triangular(cholesky_lower, identity, lower=True)


def contract_first(left, right):
    return lax.dot_general(
        left, right, (((0,), (0,)), ((), ())), precision=HIGHEST, preferred_element_type=jnp.float32
    )


def times_inverse(left, inverse):
    return jnp.dot(left, inverse.T, precision=HIGHEST, preferred_element_type=jnp.float32)


def on_device(gradient, feedback, warm_start, master, moment, second):
    replicas = lax.axis_size("rep")
    merged = gradient[0].astype(jnp.float32) + feedback[0].astype(jnp.float32)
    local_factor = contract_first(merged, warm_start)
    factor = lax.psum(local_factor, "rep") / replicas
    gram_part = contract_first(factor, factor)
    gram = lax.psum(gram_part, "shard")
    inverse = lower_inverse(gram)
    unit_basis = times_inverse(factor, inverse)
    projected = jnp.dot(merged, unit_basis, precision=HIGHEST, preferred_element_type=jnp.float32)
    right_factor = lax.psum(projected, ("rep", "shard")) / replicas
    approx = lax.dot_general(
        right_factor,
        unit_basis,
        (((1,), (1,)), ((), ())),
        precision=HIGHEST,
        preferred_element_type=jnp.float32,
    )
    new_feedback = (merged - approx).astype(jnp.bfloat16)[None]
    own_rows = master.shape[0]
    row_start = lax.axis_index("rep") * own_rows
    grad_rows = lax.dynamic_slice_in_dim(approx, row_start, own_rows, 0)
    moment_out = beta_one * moment + (1.0 - beta_one) * grad_rows
    second_out = beta_two * second + (1.0 - beta_two) * grad_rows * grad_rows
    master_out = master - learn_rate * (
        moment_out / (jnp.sqrt(second_out) + adam_eps) + decay_rate * master
    )
    weights = lax.all_gather(master_out.astype(jnp.bfloat16), "rep", axis=0, tiled=True)
    return (new_feedback, weights, master_out, moment_out, second_out, right_factor)


def solution(mesh):
    return jax.shard_map(
        on_device,
        mesh=mesh,
        in_specs=(
            P("rep", None, "shard"),
            P("rep", None, "shard"),
            P(),
            P("rep", "shard"),
            P("rep", "shard"),
            P("rep", "shard"),
        ),
        out_specs=(
            P("rep", None, "shard"),
            P(None, "shard"),
            P("rep", "shard"),
            P("rep", "shard"),
            P("rep", "shard"),
            P(),
        ),
        check_vma=False,
    )
```

profile of v0, /device:TPU:2, one launch (start us, length us, event | category | flops | bytes accessed | tf_op | source)
XLA Modules:
  0.0 533.7 jit_solution(15276774667782180067)
XLA Ops:
  7.2 0.0 copy-start
  7.2 0.0 copy-start.1
  7.2 0.0 all-reduce.3.cloned.1.call-start
  7.2 0.9 copy-done
  8.1 3.8 fusion.2
  12.0 0.0 all-reduce.3.cloned.1.call-update
  12.0 0.0 all-reduce.5.cloned.1.call-start
  12.0 143.7 %all-reduce.3.cloned.1.call-done = f32[512,64]{0,1:T(8,128)} async-done(((f32[512,64]{0,1:T(8,128)}), f32[512,64]{0,1:T(8,128)}) %all-reduce.3.cloned.1.call-update) | async-done | bytes 131088 | tf_op jit(solution)/shard_map/psum | solution.py:37
  155.8 1.2 fusion.8
  157.0 20.7 %psum.22 = f32[64,64]{1,0:T(8,128)S(1)} all-reduce(f32[64,64]{1,0:T(8,128)S(1)} %fusion.8), channel_id=1, replica_groups=mesh['rep'=32,'shard'=8] {'shard'}, use_global_device_ids=true, to_apply=%region_1.0 | all-reduce | flops 4096 | bytes 32768 | tf_op jit(solution)/shard_map/psum | solution.py:39
  177.7 0.6 select_reduce_fusion.1
  179.0 0.1 copy.12
  179.1 5.8 %cholesky.18 = f32[64,64]{1,0:T(8,128)S(1)} custom-call(f32[64,64]{1,0:T(8,128)S(1)} %fusion.16), custom_call_target="Cholesky" | custom-call | tf_op jit(solution)/shard_map/jit(cholesky)/cholesky | solution.py:19
  185.0 0.6 compare_reduce_fusion
  185.6 0.7 fusion.13
  186.3 4.9 custom-call.7
  191.2 0.2 fusion.14
  191.4 1.2 fusion.6
  192.6 3.0 fusion
  195.6 0.0 all-reduce.5.cloned.1.call-update
  195.7 0.0 all-gather.2.cloned.1.call-start
  195.7 249.2 %all-reduce.5.cloned.1.call-done = f32[1024,64]{0,1:T(8,128)} async-done(((f32[1024,64]{0,1:T(8,128)}), f32[1024,64]{0,1:T(8,128)}) %all-reduce.5.cloned.1.call-update) | async-done | bytes 262160 | tf_op jit(solution)/shard_map/psum | solution.py:43
  444.9 1.0 broadcast_multiply_fusion
  445.9 0.0 copy-start.4
  445.9 1.8 fusion.21
  447.8 1.3 copy-done.3
  449.1 0.0 copy-done.6
  449.1 0.7 fusion.19
  449.8 0.0 all-gather.2.cloned.1.call-update
  449.9 3.0 fusion.5
  452.9 72.0 %all-gather.2.cloned.1.call-done = bf16[1024,512]{1,0:T(8,128)(2,1)} async-done(((bf16[32,512]{1,0:T(8,128)(2,1)}), bf16[1024,512]{1,0:T(8,128)(2,1)}) %all-gather.2.cloned.1.call-update) | async-done | bytes 1048592 | tf_op jit(solution)/shard_map/all_gather | solution.py:60
  524.9 2.3 copy.16
  (13 shorter events, 0.1 us)
Async XLA Ops:
  7.2 1.0 copy-start
  7.2 185.4 %copy-start.1 = (bf16[1,1024,512]{2,1,0:T(8,128)(2,1)S(1)}, bf16[1,1024,512]{2,1,0:T(8,128)(2,1)}, u32[]{:S(2)}) copy-start(bf16[1,1024,512]{2,1,0:T(8,128)(2,1)} %param.7) | copy-start | bytes 3145732
  7.2 185.4 %copy-start.2 = (bf16[1,1024,512]{2,1,0:T(8,128)(2,1)S(1)}, bf16[1,1024,512]{2,1,0:T(8,128)(2,1)}, u32[]{:S(2)}) copy-start(bf16[1,1024,512]{2,1,0:T(8,128)(2,1)} %param.6) | copy-start | bytes 3145732
  7.2 148.6 %all-reduce.3.cloned.1.call-start = ((), (), s32[]{:S(2)}) async-start(), calls=%async_computation | async-start | bytes 262144 | tf_op jit(solution)/shard_map/psum | solution.py:37
  12.0 432.9 %all-reduce.5.cloned.1.call-start = ((), (), s32[]{:S(2)}) async-start(), calls=%async_computation.1 | async-start | bytes 524288 | tf_op jit(solution)/shard_map/psum | solution.py:43
  195.6 253.5 %copy-start.5 = (f32[32,512]{1,0:T(8,128)S(1)}, f32[32,512]{1,0:T(8,128)}, u32[]{:S(2)}) copy-start(f32[32,512]{1,0:T(8,128)} %param.9) | copy-start | bytes 196612
  195.6 253.5 %copy-start.6 = (f32[32,512]{1,0:T(8,128)S(1)}, f32[32,512]{1,0:T(8,128)}, u32[]{:S(2)}) copy-start(f32[32,512]{1,0:T(8,128)} %param.11) | copy-start | bytes 196612
  195.6 253.5 %copy-start.7 = (f32[32,512]{1,0:T(8,128)S(1)}, f32[32,512]{1,0:T(8,128)}, u32[]{:S(2)}) copy-start(f32[32,512]{1,0:T(8,128)} %param.10) | copy-start | bytes 196612
  195.7 329.2 %all-gather.2.cloned.1.call-start = ((), (), s32[]{:S(2)}) async-start(), calls=%async_computation.2 | async-start | bytes 1081344 | tf_op jit(solution)/shard_map/all_gather | solution.py:60
  445.9 7.0 %copy-start.4 = (f32[1024,64]{0,1:T(8,128)}, f32[1024,64]{0,1:T(8,128)S(1)}, u32[]{:S(2)}) copy-start(f32[1024,64]{0,1:T(8,128)S(1)} %broadcast_multiply_fusion) | copy-start | bytes 786436
  447.8 1.3 copy-start.3
Sparse Core Ops, SparseCore 0:
  12.1 143.6 all-reduce.2
  195.8 249.0 all-reduce.4
  450.0 74.8 all-gather.1
where the time goes:
time: 534 us
  waiting for transfers between devices  465 us (87%)
  blocking collectives  20.7 us (4%)
  other arithmetic  17.4 us (3%)
  between operations  14.5 us (3%)
  matrix products  11.4 us (2%)
    psum x1, waiting for transfers between devices, on_device(): right_factor = lax.psum(projected, ('rep', 'shard')) / replicas  249 us
    psum x1, waiting for transfers between devices, on_device(): factor = lax.psum(local_factor, 'rep') / replicas  144 us
    all_gather x1, waiting for transfers between devices, on_device(): lax.all_gather(master_out.astype(jnp.bfloat16), 'rep', axis=0, tiled=True)  72 us
    psum x1, blocking collectives, on_device(): gram = lax.psum(gram_part, 'shard')  20.7 us
  transfers between devices with their start and end apart: 3, of which 3 were waited for; matrix products, arithmetic and copies ran while one was open for 1% of the time, Pallas kernels for 0%

commit v1 on v0

--- a/solution.py
+++ b/solution.py
@@ -10,6 +10,14 @@
 decay_rate = 0.1
 adam_eps = 1e-08
 ridge_rate = 1e-06
+
+
+def _save_heads(frame_in):
+    comm_axis = "rep"
+    net_axis = "shard"
+    for j in (net_axis, comm_axis):
+        frame_in = lax.psum(frame_in, j)
+    return frame_in
 
 
 def lower_inverse(gram):
@@ -40,7 +48,7 @@
     inverse = lower_inverse(gram)
     unit_basis = times_inverse(factor, inverse)
     projected = jnp.dot(merged, unit_basis, precision=HIGHEST, preferred_element_type=jnp.float32)
-    right_factor = lax.psum(projected, ("rep", "shard")) / replicas
+    right_factor = _save_heads(projected) / replicas
     approx = lax.dot_general(
         right_factor,
         unit_basis,

time: 534 us -> 494 us (0.925)
  waiting for transfers between devices: 465 us -> 425 us
    psum x1 -> x2, waiting for transfers between devices: 249 us -> 211 us  [_save_heads(): frame_in = lax.psum(frame_in, j)]
  transfers between devices with their start and end apart: 3 -> 4, of which waited for: 3 -> 4; matrix products, arithmetic and copies ran while one was open for 1% -> 1% of each run, Pallas kernels for 0% -> 0%
where the time goes in v1:
time: 494 us; the launch traced here: 493 us
  waiting for transfers between devices  425 us (86%)
  blocking collectives  20.7 us (4%)
  other arithmetic  17.4 us (4%)
  between operations  14.5 us (3%)
  matrix products  11.4 us (2%)
    psum x2, waiting for transfers between devices, _save_heads(): frame_in = lax.psum(frame_in, j)  211 us
    psum x1, waiting for transfers between devices, on_device(): factor = lax.psum(local_factor, 'rep') / replicas  144 us
    all_gather x1, waiting for transfers between devices, on_device(): lax.all_gather(master_out.astype(jnp.bfloat16), 'rep', axis=0, tiled=True)  70.3 us
    psum x1, blocking collectives, on_device(): gram = lax.psum(gram_part, 'shard')  20.7 us
  transfers between devices with their start and end apart: 4, of which 4 were waited for; matrix products, arithmetic and copies ran while one was open for 1% of the time, Pallas kernels for 0%

profile of v1, /device:TPU:2, one launch (start us, length us, event | category | flops | bytes accessed | tf_op | source)
XLA Modules:
  0.0 493.3 jit_solution(8741388548655898110)
XLA Ops:
  7.2 0.0 copy-start
  7.2 0.0 all-reduce.4.cloned.1.call-start
  7.2 0.9 copy-done
  8.1 3.8 fusion.2
  12.0 0.0 all-reduce.4.cloned.1.call-update
  12.0 0.0 all-reduce.6.cloned.1.call-start
  12.0 143.7 %all-reduce.4.cloned.1.call-done = f32[512,64]{0,1:T(8,128)} async-done(((f32[512,64]{0,1:T(8,128)}), f32[512,64]{0,1:T(8,128)}) %all-reduce.4.cloned.1.call-update) | async-done | bytes 131088 | tf_op jit(solution)/shard_map/psum | solution.py:45
  155.8 1.2 fusion.8
  157.0 20.7 %psum.29 = f32[64,64]{1,0:T(8,128)S(1)} all-reduce(f32[64,64]{1,0:T(8,128)S(1)} %fusion.8), channel_id=1, replica_groups=mesh['rep'=32,'shard'=8] {'shard'}, use_global_device_ids=true, to_apply=%region_1.0 | all-reduce | flops 4096 | bytes 32768 | tf_op jit(solution)/shard_map/psum | solution.py:47
  177.7 0.6 select_reduce_fusion.1
  179.0 0.1 copy.12
  179.1 5.8 %cholesky.18 = f32[64,64]{1,0:T(8,128)S(1)} custom-call(f32[64,64]{1,0:T(8,128)S(1)} %fusion.16), custom_call_target="Cholesky" | custom-call | tf_op jit(solution)/shard_map/jit(cholesky)/cholesky | solution.py:27
  185.0 0.6 compare_reduce_fusion
  185.6 0.7 fusion.13
  186.3 4.9 custom-call.7
  191.2 0.2 fusion.14
  191.4 1.2 fusion.6
  192.6 3.0 fusion
  195.6 0.0 all-reduce.6.cloned.1.call-update
  195.7 0.0 all-reduce.8.cloned.1.call-start
  195.7 61.6 %all-reduce.6.cloned.1.call-done = f32[1024,64]{0,1:T(8,128)} async-done(((f32[1024,64]{0,1:T(8,128)}), f32[1024,64]{0,1:T(8,128)}) %all-reduce.6.cloned.1.call-update) | async-done | bytes 262160 | tf_op jit(solution)/shard_map/psum | solution.py:19
  257.3 0.0 all-reduce.8.cloned.1.call-update
  257.3 0.0 all-gather.2.cloned.1.call-start
  257.4 148.9 %all-reduce.8.cloned.1.call-done = f32[1024,64]{0,1:T(8,128)} async-done(((f32[1024,64]{0,1:T(8,128)}), f32[1024,64]{0,1:T(8,128)}) %all-reduce.8.cloned.1.call-update) | async-done | bytes 262160 | tf_op jit(solution)/shard_map/psum | solution.py:19
  406.3 1.0 broadcast_multiply_fusion
  407.3 1.8 fusion.21
  409.2 1.3 copy-done.3
  410.5 0.7 fusion.19
  411.2 0.0 all-gather.2.cloned.1.call-update
  411.2 3.0 fusion.5
  414.3 70.3 %all-gather.2.cloned.1.call-done = bf16[1024,512]{1,0:T(8,128)(2,1)} async-done(((bf16[32,512]{1,0:T(8,128)(2,1)}), bf16[1024,512]{1,0:T(8,128)(2,1)}) %all-gather.2.cloned.1.call-update) | async-done | bytes 1048592 | tf_op jit(solution)/shard_map/all_gather | solution.py:68
  484.5 2.3 copy.17
  (16 shorter events, 0.1 us)
Async XLA Ops:
  7.2 1.0 copy-start
  7.2 185.4 %copy-start.1 = (bf16[1,1024,512]{2,1,0:T(8,128)(2,1)S(1)}, bf16[1,1024,512]{2,1,0:T(8,128)(2,1)}, u32[]{:S(2)}) copy-start(bf16[1,1024,512]{2,1,0:T(8,128)(2,1)} %param.7) | copy-start | bytes 3145732
  7.2 185.4 %copy-start.2 = (bf16[1,1024,512]{2,1,0:T(8,128)(2,1)S(1)}, bf16[1,1024,512]{2,1,0:T(8,128)(2,1)}, u32[]{:S(2)}) copy-start(bf16[1,1024,512]{2,1,0:T(8,128)(2,1)} %param.6) | copy-start | bytes 3145732
  7.2 148.6 %all-reduce.4.cloned.1.call-start = ((), (), s32[]{:S(2)}) async-start(), calls=%async_computation | async-start | bytes 262144 | tf_op jit(solution)/shard_map/psum | solution.py:45
  12.0 245.3 %all-reduce.6.cloned.1.call-start = ((), (), s32[]{:S(2)}) async-start(), calls=%async_computation.1 | async-start | bytes 524288 | tf_op jit(solution)/shard_map/psum | solution.py:19
  195.6 214.9 %copy-start.5 = (f32[32,512]{1,0:T(8,128)S(1)}, f32[32,512]{1,0:T(8,128)}, u32[]{:S(2)}) copy-start(f32[32,512]{1,0:T(8,128)} %param.9) | copy-start | bytes 196612
  195.6 214.9 %copy-start.6 = (f32[32,512]{1,0:T(8,128)S(1)}, f32[32,512]{1,0:T(8,128)}, u32[]{:S(2)}) copy-start(f32[32,512]{1,0:T(8,128)} %param.11) | copy-start | bytes 196612
  195.6 214.9 %copy-start.7 = (f32[32,512]{1,0:T(8,128)S(1)}, f32[32,512]{1,0:T(8,128)}, u32[]{:S(2)}) copy-start(f32[32,512]{1,0:T(8,128)} %param.10) | copy-start | bytes 196612
  195.7 210.6 %all-reduce.8.cloned.1.call-start = ((), (), s32[]{:S(2)}) async-start(), calls=%async_computation.2 | async-start | bytes 524288 | tf_op jit(solution)/shard_map/psum | solution.py:19
  257.3 227.2 %all-gather.2.cloned.1.call-start = ((), (), s32[]{:S(2)}) async-start(), calls=%async_computation.3 | async-start | bytes 1081344 | tf_op jit(solution)/shard_map/all_gather | solution.py:68
  407.3 7.0 %copy-start.4 = (f32[1024,64]{0,1:T(8,128)}, f32[1024,64]{0,1:T(8,128)S(1)}, u32[]{:S(2)}) copy-start(f32[1024,64]{0,1:T(8,128)S(1)} %broadcast_multiply_fusion) | copy-start | bytes 786436
  409.2 1.3 copy-start.3
Sparse Core Ops, SparseCore 0:
  12.1 143.6 all-reduce.3
  195.8 61.4 all-reduce.5
  260.8 145.4 all-reduce.7
  411.4 73.1 all-gather.1
